TPU v7x, 32 devices: a whole 2x2x4 slice. The times are simulated.
32 devices in a mesh: dp: 8 (over z, y), tensor: 4 (over x, core).
Axes of the slice: x: 2, y: 2, z: 4, core: 2. Of those that a mesh axis runs over, the one named last changes fastest.
Arguments:
- query_act: bfloat16 [8, 1024, 1024], P('dp', None, 'tensor'), may hold values from -6 to 6
- rotated_keys: bfloat16 [8, 1024, 256], P('dp'), may hold values from -6 to 6
- value_input: bfloat16 [8, 1024, 256], P('dp'), may hold values from -6 to 6
- grad_out: bfloat16 [8, 1024, 8192], P('dp', 'tensor'), may hold values from -6 to 6
- out_weight: bfloat16 [1024, 8192], P('tensor', 'dp'), may hold values from -0.1875 to 0.1875
- doc_lengths: int32 [8, 4], P('dp'), may hold values from 1 to 512, 1024 in all within a row
Outputs:
- query_grad: bfloat16 [8, 1024, 1024], P('dp', None, 'tensor')
- key_gradient: bfloat16 [8, 4, 512, 128], P('dp', 'tensor')
- value_gradient: bfloat16 [8, 4, 512, 128], P('dp', 'tensor')
- weight_grad: float32 [1024, 8192], P('tensor', 'dp')
All inputs are finite; a program needn't handle non-finite values.
Results may differ from a plain program's by a relative error of at most 0.015.
The roundings to bfloat16 on the way count: a program that leaves them out, or rounds other values in their place, can miss the bound.
Values may be sent and summed in bfloat16 or wider, within the bound.
A program may use at most 128 MiB of HBM per device.

v0:
```python
import jax
import jax.numpy as jnp
from jax import lax
from jax.sharding import PartitionSpec as P

HEAD_SIZE = 128


def swapped(value, axis, apart):
    mask = 2**apart
    pairs = [(source, source ^ mask) for source in range(lax.axis_size(axis))]
    return lax.ppermute(value, axis, pairs)


def shards(query_act, rotated_keys, value_input, grad_out, out_weight, doc_lengths):
    score_scale = HEAD_SIZE ** (-0.5)
    tensor_index = lax.axis_index("tensor")
    kv_group = tensor_index // 2
    own_half = tensor_index % 2
    seq_len = query_act.shape[1]
    head_count = query_act.shape[2] // HEAD_SIZE
    query_heads = query_act[0].reshape(seq_len, head_count, HEAD_SIZE).transpose(1, 0, 2)
    key_rows = lax.dynamic_slice_in_dim(rotated_keys[0], kv_group * HEAD_SIZE, HEAD_SIZE, 1)
    value_rows = lax.dynamic_slice_in_dim(value_input[0], kv_group * HEAD_SIZE, HEAD_SIZE, 1)
    doc_ends = jnp.cumsum(doc_lengths[0])
    positions = jnp.arange(seq_len, dtype=jnp.int32)
    doc_ids = jnp.sum((positions[:, None] >= doc_ends[None, :]).astype(jnp.int32), axis=1)
    block_rows = min(512, seq_len)
    block_count = seq_len // block_rows
    full_weight = lax.all_gather(out_weight, "dp", axis=1, tiled=True)

    def key_reach():
        return seq_len

    def masked_scores(block_idx, key_span):
        first = block_idx * block_rows
        query_block = query_heads[:, first : first + block_rows]
        scores = (
            jnp.einsum("hqd,kd->hqk", query_block, key_rows, preferred_element_type=jnp.float32)
            * score_scale
        )
        allowed = (positions[None, :key_span] <= positions[first : first + block_rows, None]) & (
            doc_ids[None, :key_span] == doc_ids[first : first + block_rows, None]
        )
        return jnp.where(allowed[None], scores, -jnp.inf)

    totals_list = []
    outputs_list = []
    for block_idx in range(block_count):
        key_span = key_reach()
        scores = masked_scores(block_idx, key_span)
        row_max = jnp.max(scores, axis=-1, keepdims=True)
        log_total = row_max + jnp.log(jnp.sum(jnp.exp(scores - row_max), axis=-1, keepdims=True))
        prob_bf16 = jnp.exp(scores - log_total).astype(jnp.bfloat16)
        outputs_list.append(
            jnp.einsum(
                "hqk,kd->hqd", prob_bf16, value_rows, preferred_element_type=jnp.float32
            ).astype(jnp.bfloat16)
        )
        totals_list.append(log_total)
    attn_out = jnp.concatenate(outputs_list, axis=1)
    out_flat = attn_out.transpose(1, 0, 2).reshape(seq_len, head_count * HEAD_SIZE)
    local_rows = grad_out[0]
    gathered = lax.all_gather(local_rows, "tensor", axis=0, tiled=True)
    out_grad = jnp.einsum(
        "sd,hd->sh", gathered, full_weight, preferred_element_type=jnp.float32
    ).astype(jnp.bfloat16)
    weight_part = jnp.einsum("sh,sd->hd", out_flat, gathered, preferred_element_type=jnp.float32)
    weight_grad = lax.psum_scatter(weight_part, "dp", scatter_dimension=1, tiled=True)
    grad_heads = out_grad.reshape(seq_len, head_count, HEAD_SIZE).transpose(1, 0, 2)
    key_accum = jnp.zeros((seq_len, HEAD_SIZE), jnp.float32)
    value_accum = jnp.zeros((seq_len, HEAD_SIZE), jnp.float32)
    query_list = []
    for block_idx in range(block_count):
        key_span = key_reach()
        first = block_idx * block_rows
        scores = masked_scores(block_idx, key_span)
        prob_block = jnp.exp(scores - totals_list[block_idx])
        prob_bf16 = prob_block.astype(jnp.bfloat16)
        grad_block = grad_heads[:, first : first + block_rows]
        out_block = attn_out[:, first : first + block_rows]
        query_block = query_heads[:, first : first + block_rows]
        dprobs = jnp.einsum(
            "hqd,kd->hqk", grad_block, value_rows, preferred_element_type=jnp.float32
        )
        row_delta = jnp.sum(
            grad_block.astype(jnp.float32) * out_block.astype(jnp.float32), axis=-1, keepdims=True
        )
        score_gradient = (prob_block * (dprobs - row_delta) * score_scale).astype(jnp.bfloat16)
        query_list.append(
            jnp.einsum(
                "hqk,kd->hqd", score_gradient, key_rows, preferred_element_type=jnp.float32
            ).astype(jnp.bfloat16)
        )
        key_accum = key_accum.at[:key_span].add(
            jnp.einsum(
                "hqk,hqd->kd", score_gradient, query_block, preferred_element_type=jnp.float32
            )
        )
        value_accum = value_accum.at[:key_span].add(
            jnp.einsum("hqk,hqd->kd", prob_bf16, grad_block, preferred_element_type=jnp.float32)
        )
    query_grad = (
        jnp.concatenate(query_list, axis=1)
        .transpose(1, 0, 2)
        .reshape(1, seq_len, head_count * HEAD_SIZE)
    )
    half_rows = seq_len // 2
    other_start = (1 - own_half) * half_rows
    outgoing = (
        lax.dynamic_slice_in_dim(key_accum, other_start, half_rows, 0),
        lax.dynamic_slice_in_dim(value_accum, other_start, half_rows, 0),
    )
    partner = swapped((outgoing[0], outgoing[1]), "tensor", 0)
    key_mine = lax.dynamic_slice_in_dim(key_accum, own_half * half_rows, half_rows, 0) + partner[0]
    value_mine = (
        lax.dynamic_slice_in_dim(value_accum, own_half * half_rows, half_rows, 0) + partner[1]
    )
    key_gradient = key_mine.astype(jnp.bfloat16).reshape(1, 1, half_rows, HEAD_SIZE)
    value_gradient = value_mine.astype(jnp.bfloat16).reshape(1, 1, half_rows, HEAD_SIZE)
    return (query_grad, key_gradient, value_gradient, weight_grad)


def solution(mesh):
    placed = (
        P("dp", None, "tensor"),
        P("dp", None, None),
        P("dp", None, None),
        P("dp", "tensor", None),
        P("tensor", "dp"),
        P("dp", None),
    )
    return jax.shard_map(
        shards,
        mesh=mesh,
        in_specs=placed,
        out_specs=(
            P("dp", None, "tensor"),
            P("dp", "tensor", None, None),
            P("dp", "tensor", None, None),
            P("tensor", "dp"),
        ),
        check_vma=False,
    )
```

profile of v0, /device:TPU:0, one launch (start us, length us, event | category | flops | bytes accessed | tf_op | source)
XLA Modules:
  0.0 374.6 jit_solution(8681585686457070649)
XLA Ops:
  8.0 0.7 all-gather.6.cloned.1.call-update
  9.6 0.9 fusion.9
  10.5 0.9 fusion.7
  11.4 0.9 fusion.6
  12.4 2.2 exponential_reduce_fusion
  14.7 1.6 convolution_convert_fusion.1
  16.2 69.5 %all-gather.4.cloned.1.call-done = bf16[256,8192]{1,0:T(8,128)(2,1)} async-done(((bf16[256,1024]{1,0:T(8,128)(2,1)}), bf16[256,8192]{1,0:T(8,128)(2,1)}) %all-gather.4.cloned.1.call-update) | async-done | bytes 4194320 | tf_op jit(solution)/shard_map/all_gather | solution.py:30
  85.7 106.0 %all-gather.6.cloned.1.call-done = bf16[1,1024,8192]{2,1,0:T(8,128)(2,1)} async-done(((bf16[1,256,8192]{2,1,0:T(8,128)(2,1)}), bf16[1,1024,8192]{2,1,0:T(8,128)(2,1)}) %all-gather.6.cloned.1.call-update) | async-done | bytes 16777232 | tf_op jit(solution)/shard_map/all_gather | solution.py:64
  191.8 11.5 %fusion.10 = bf16[1024,256]{0,1:T(8,128)(2,1)S(1)} fusion(bf16[256,8192]{1,0:T(8,128)(2,1)} %all-gather.4.cloned.1.call-done, bf16[1,1024,8192]{2,1,0:T(8,128)(2,1)} %all-gather.6.cloned.1.call-done), kind=kOutput, calls=%fused_computation.20 | convolution fusion | flops 4295229440 | bytes 21495808 | tf_op jit(solution)/shard_map/sd,hd->sh/dot_general | solution.py:65
  203.5 3.8 %multiply_reduce_fusion.1 = (f32[2,512]{1,0:T(2,128)S(1)}, f32[2,512]{1,0:T(2,128)S(1)}, bf16[2,512,128]{2,1,0:T(8,128)(2,1)S(1)}) fusion(bf16[2,1024,128]{2,1,0:T(8,128)(2,1)S(1)} %bitcast.100, bf16[2,512,128]{2,1,0:T(8,128)(2,1)S(1)} %convolution_convert_fusion.1, bf16[1,1024,256]{2,1,0:T(8,128)(2,1)S(1)} %copy-done, s32[]{:T(128)S(6)} %select_n.33, ...), kind=kOutput, calls=%fused_computation.34 | convolution fusion | flops 273807360 | bytes 6041604 | tf_op jit(solution)/shard_map/hqk,kd->hqd/dot_general | solution.py:56
  207.6 12.5 %fusion = f32[256,8192]{1,0:T(8,128)} fusion(bf16[1024,256]{0,1:T(8,128)(2,1)S(1)} %bitcast.93, bf16[1,1024,8192]{2,1,0:T(8,128)(2,1)} %all-gather.6.cloned.1.call-done), kind=kOutput, calls=%fused_computation | convolution fusion | flops 4294967296 | bytes 25690112 | tf_op jit(solution)/shard_map/sh,sd->hd/dot_general | solution.py:68
  220.1 1.0 copy-done.7
  221.1 4.0 %multiply_convert_fusion = bf16[2,512,1024]{1,2,0:T(8,128)(2,1)S(1)} fusion(f32[1024,2,512]{2,0,1:T(8,128)} %copy-done.1, f32[2,512]{1,0:T(2,128)S(1)} %get-tuple-element.93, f32[2,512]{1,0:T(2,128)S(1)} %log_add_fusion, pred[512,1024]{0,1:T(8,128)(4,1)S(1)} %get-tuple-element.94, bf16[2,1024,128]{2,1,0:T(8,128)(2,1)S(1)} %bitcast.101, ...), kind=kOutput, calls=%fused_computation.6 | convolution fusion | flops 275775488 | bytes 7348228 | tf_op jit(solution)/shard_map/hqd,kd->hqk/dot_general | solution.py:83
  225.1 0.7 convolution_bitcast_fusion.2
  225.8 1.7 multiply_convert_fusion.1
  227.5 0.7 fusion.13
  228.6 0.8 convolution_convert_fusion
  229.8 1.1 convolution_bitcast_fusion
  230.8 1.3 fusion.14
  232.1 0.8 convolution_convert_fusion.2
  233.5 1.0 copy.40
  234.5 0.7 fusion.41
  235.2 1.6 fusion.42
  236.8 131.3 %reduce-scatter.2.cloned.1.call-done = f32[256,1024]{1,0:T(8,128)} async-done(((f32[256,8192]{1,0:T(8,128)}), f32[256,1024]{1,0:T(8,128)}) %reduce-scatter.2.cloned.1.call-update) | async-done | bytes 1048592 | tf_op jit(solution)/shard_map/reduce_scatter | solution.py:69
  (48 shorter events, 3.6 us)
Async XLA Ops:
  7.2 7.5 %copy-start = (bf16[1,1024,256]{2,1,0:T(8,128)(2,1)S(1)}, bf16[1,1024,256]{2,1,0:T(8,128)(2,1)}, u32[]{:S(2)}) copy-start(bf16[1,1024,256]{2,1,0:T(8,128)(2,1)} %param.24) | copy-start | bytes 1572868
  7.2 1.6 copy-start.10
  7.2 1.8 copy-start.5
  7.2 3.3 copy-start.8
  7.2 78.5 %all-gather.4.cloned.1.call-start = ((), (), s32[]{:S(2)}) async-start(), calls=%async_computation.1 | async-start | bytes 4718592 | tf_op jit(solution)/shard_map/all_gather | solution.py:30
  7.9 183.8 %all-gather.6.cloned.1.call-start = ((), (), s32[]{:S(2)}) async-start(), calls=%async_computation.3 | async-start | bytes 20971520 | tf_op jit(solution)/shard_map/all_gather | solution.py:64
  8.7 359.4 %reduce-scatter.2.cloned.1.call-start = ((), (), s32[]{:S(2)}) async-start(), calls=%async_computation.2 | async-start | bytes 9437184 | tf_op jit(solution)/shard_map/reduce_scatter | solution.py:69
  11.4 3.2 copy-start.1
  12.4 2.3 copy-start.3
  203.5 3.8 %copy-start.6 = (bf16[1024,2,128]{2,0,1:T(8,128)(2,1)}, bf16[1024,2,128]{2,0,1:T(8,128)(2,1)S(1)}, u32[]{:S(2)}) copy-start(bf16[1024,2,128]{2,0,1:T(8,128)(2,1)S(1)} %copy.31) | copy-start | bytes 1572868
  220.1 1.0 copy-start.7
  221.1 4.7 %copy-start.4 = (f32[1024,2,512]{2,0,1:T(8,128)S(1)}, f32[1024,2,512]{2,0,1:T(8,128)}, u32[]{:S(2)}) copy-start(f32[1024,2,512]{2,0,1:T(8,128)} %copy-done.3) | copy-start | bytes 12582916
  225.8 2.8 copy-start.9
  227.5 2.3 copy-start.2
  228.3 6.2 %collective-permute-start = (f32[512,128]{1,0:T(8,128)S(1)}, f32[512,128]{1,0:T(8,128)S(1)}, u32[]{:S(2)}, u32[]{:S(2)}) collective-permute-start(f32[512,128]{1,0:T(8,128)S(1)} %constant_dynamic-slice_fusion.1), channel_id=1, source_target_pairs={{0,1},{1,0},{2,3},{3,2},{4,5},{5,4},{6,7},{7,6},{8,9},{9,8},{10,11... | collective-permute-start | bytes 786440 | tf_op jit(solution)/shard_map/ppermute | solution.py:12
  232.9 2.3 collective-permute-start.1
Sparse Core Ops, SparseCore 0:
  10.2 75.4 all-gather.3
  87.3 104.4 all-gather.5
  220.2 147.8 reduce-scatter.1
where the time goes:
time: 375 us
  waiting for transfers between devices  308 us (82%)
  matrix products  42.1 us (11%)
  between operations  14.1 us (4%)
  other arithmetic  5.72 us (2%)
  local copies, waits for them, and re-layouts  3.8 us (1%)
    reduce_scatter x1, waiting for transfers between devices, shards(): lax.psum_scatter(weight_part, 'dp', scatter_dimension=1, tiled=True)  131 us
    all_gather x1, waiting for transfers between devices, shards(): gathered = lax.all_gather(local_rows, 'tensor', axis=0, tiled=True)  106 us
    all_gather x1, waiting for transfers between devices, shards(): full_weight = lax.all_gather(out_weight, 'dp', axis=1, tiled=True)  69.5 us
    dot_general x1, matrix products, shards(): jnp.einsum('sh,sd->hd', out_flat, gathered, preferred_element_type=jnp.fl...  12.5 us
    dot_general x1, matrix products, shards(): jnp.einsum('sd,hd->sh', gathered, full_weight, preferred_element_type=jnp...  11.5 us
  transfers between devices with their start and end apart: 5, of which 3 were waited for; matrix products, arithmetic and copies ran while one was open for 6% of the time, Pallas kernels for 0%

commit v1 on v0

--- a/solution.py
+++ b/solution.py
@@ -4,6 +4,18 @@
 from jax.sharding import PartitionSpec as P
 
 HEAD_SIZE = 128
+
+
+def summed_around(shard, axis, dim, term):
+    size, position, span = (lax.axis_size(axis), lax.axis_index(axis), shard.shape[dim])
+    upward = [(i, (i + 1) % size) for i in range(size)]
+    held, subtotal = (shard, None)
+    for step in range(size):
+        coming = lax.ppermute(held, axis, upward) if step < size - 1 else None
+        absorb = term(held, (position - step) % size * span)
+        subtotal = absorb if subtotal is None else subtotal + absorb
+        held = coming
+    return subtotal
 
 
 def swapped(value, axis, apart):
@@ -27,7 +39,6 @@
     doc_ids = jnp.sum((positions[:, None] >= doc_ends[None, :]).astype(jnp.int32), axis=1)
     block_rows = min(512, seq_len)
     block_count = seq_len // block_rows
-    full_weight = lax.all_gather(out_weight, "dp", axis=1, tiled=True)
 
     def key_reach():
         return seq_len
@@ -62,8 +73,16 @@
     out_flat = attn_out.transpose(1, 0, 2).reshape(seq_len, head_count * HEAD_SIZE)
     local_rows = grad_out[0]
     gathered = lax.all_gather(local_rows, "tensor", axis=0, tiled=True)
-    out_grad = jnp.einsum(
-        "sd,hd->sh", gathered, full_weight, preferred_element_type=jnp.float32
+    out_grad = summed_around(
+        out_weight,
+        "dp",
+        1,
+        lambda shard, offset: jnp.einsum(
+            "sd,hd->sh",
+            lax.dynamic_slice_in_dim(gathered, offset, shard.shape[1], axis=1),
+            shard,
+            preferred_element_type=jnp.float32,
+        ),
     ).astype(jnp.bfloat16)
     weight_part = jnp.einsum("sh,sd->hd", out_flat, gathered, preferred_element_type=jnp.float32)
     weight_grad = lax.psum_scatter(weight_part, "dp", scatter_dimension=1, tiled=True)

time: 375 us -> 308 us (0.82)
  waiting for transfers between devices: 308 us -> 227 us
  matrix products: 42.1 us -> 52.4 us
    all_gather x1, waiting for transfers between devices: 106 us -> 20.9 us  [shards(): gathered = lax.all_gather(local_rows, 'tensor', axis=0, tiled=True)]
    ppermute x0 -> x7, waiting for transfers between devices: none -> 74.4 us  [summed_around(): coming = lax.ppermute(held, axis, upward) if step < size - 1 else None]
    all_gather x1 -> x0, waiting for transfers between devices: 69.5 us -> none  [shards(): full_weight = lax.all_gather(out_weight, 'dp', axis=1, tiled=True)]
    dot_general x1 -> x8, matrix products: 11.5 us -> 17.3 us  [shards(): jnp.einsum('sd,hd->sh', lax.dynamic_slice_in_dim(gathered, offset, shard....]
  transfers between devices with their start and end apart: 5 -> 11, of which waited for: 3 -> 8; matrix products, arithmetic and copies ran while one was open for 6% -> 13% of each run, Pallas kernels for 0% -> 0%
where the time goes in v1:
time: 308 us
  waiting for transfers between devices  227 us (74%)
  matrix products  52.4 us (17%)
  between operations  14.6 us (5%)
  other arithmetic  5.53 us (2%)
  local copies, waits for them, and re-layouts  4.01 us (1%)
  starting transfers between devices  3.74 us (1%)
    reduce_scatter x1, waiting for transfers between devices, shards(): lax.psum_scatter(weight_part, 'dp', scatter_dimension=1, tiled=True)  131 us
    ppermute x7, waiting for transfers between devices, summed_around(): coming = lax.ppermute(held, axis, upward) if step < size - 1 else None  74.4 us
    all_gather x1, waiting for transfers between devices, shards(): gathered = lax.all_gather(local_rows, 'tensor', axis=0, tiled=True)  20.9 us
    dot_general x8, matrix products, shards(): jnp.einsum('sd,hd->sh', lax.dynamic_slice_in_dim(gathered, offset, shard....  17.3 us
    dot_general x1, matrix products, shards(): jnp.einsum('sh,sd->hd', out_flat, gathered, preferred_element_type=jnp.fl...  12.7 us
    dot_general x2, matrix products, shards(): jnp.einsum('hqk,kd->hqd', prob_bf16, value_rows, preferred_element_type=j...  7.51 us
  transfers between devices with their start and end apart: 11, of which 8 were waited for; matrix products, arithmetic and copies ran while one was open for 13% of the time, Pallas kernels for 0%

profile of v1, /device:TPU:0, one launch (start us, length us, event | category | flops | bytes accessed | tf_op | source)
XLA Modules:
  0.0 307.7 jit_solution(11136758762622145101)
XLA Ops:
  8.3 3.0 collective-permute-start
  11.3 15.0 %collective-permute-done = bf16[256,1024]{1,0:T(8,128)(2,1)S(1)} collective-permute-done((bf16[256,1024]{1,0:T(8,128)(2,1)S(1)}, bf16[256,1024]{1,0:T(8,128)(2,1)S(1)}, u32[]{:S(2)}, u32[]{:S(2)}) %collective-permute-start) | collective-permute-done | bytes 524320 | tf_op jit(solution)/shard_map/ppermute | solution.py:14
  27.0 15.1 %collective-permute-done.1 = bf16[256,1024]{1,0:T(8,128)(2,1)} collective-permute-done((bf16[256,1024]{1,0:T(8,128)(2,1)S(1)}, bf16[256,1024]{1,0:T(8,128)(2,1)}, u32[]{:S(2)}, u32[]{:S(2)}) %collective-permute-start.1) | collective-permute-done | bytes 524320 | tf_op jit(solution)/shard_map/ppermute | solution.py:14
  43.0 14.2 %collective-permute-done.2 = bf16[256,1024]{1,0:T(8,128)(2,1)S(1)} collective-permute-done((bf16[256,1024]{1,0:T(8,128)(2,1)}, bf16[256,1024]{1,0:T(8,128)(2,1)S(1)}, u32[]{:S(2)}, u32[]{:S(2)}) %collective-permute-start.2) | collective-permute-done | bytes 524320 | tf_op jit(solution)/shard_map/ppermute | solution.py:14
  57.3 1.9 fusion.5
  59.2 2.1 fusion.4
  61.2 10.1 %collective-permute-done.3 = bf16[256,1024]{1,0:T(8,128)(2,1)S(1)} collective-permute-done((bf16[256,1024]{1,0:T(8,128)(2,1)S(1)}, bf16[256,1024]{1,0:T(8,128)(2,1)S(1)}, u32[]{:S(2)}, u32[]{:S(2)}) %collective-permute-start.3) | collective-permute-done | bytes 524320 | tf_op jit(solution)/shard_map/ppermute | solution.py:14
  71.3 2.0 exponential_reduce_fusion
  73.4 11.3 %collective-permute-done.4 = bf16[256,1024]{1,0:T(8,128)(2,1)} collective-permute-done((bf16[256,1024]{1,0:T(8,128)(2,1)S(1)}, bf16[256,1024]{1,0:T(8,128)(2,1)}, u32[]{:S(2)}, u32[]{:S(2)}) %collective-permute-start.4) | collective-permute-done | bytes 524320 | tf_op jit(solution)/shard_map/ppermute | solution.py:14
  84.9 3.7 %convolution_convert_fusion.1 = bf16[2,512,128]{2,1,0:T(8,128)(2,1)S(1)} fusion(bf16[1,1024,256]{2,1,0:T(8,128)(2,1)S(1)} %copy-done, s32[]{:T(128)S(6)} %select_n.89, f32[1024,2,512]{2,0,1:T(8,128)} %copy-done.2, f32[2,512]{1,0:T(2,128)S(1)} %log_add_fusion, pred[512,1024]{0,1:T(8,128)(4,1)S(1)} %get-tuple-element.94), kind=kOutput, calls=%fused_computation.57 | convolution fusion | flops 272760832 | bytes 5246980 | tf_op jit(solution)/shard_map/hqk,kd->hqd/dot_general | solution.py:67
  88.6 8.8 %collective-permute-done.5 = bf16[256,1024]{1,0:T(8,128)(2,1)} collective-permute-done((bf16[256,1024]{1,0:T(8,128)(2,1)}, bf16[256,1024]{1,0:T(8,128)(2,1)}, u32[]{:S(2)}, u32[]{:S(2)}) %collective-permute-start.5) | collective-permute-done | bytes 524320 | tf_op jit(solution)/shard_map/ppermute | solution.py:14
  97.3 20.9 %all-gather.3.cloned.1.call-done = bf16[1,1024,8192]{2,1,0:T(8,128)(2,1)} async-done(((bf16[1,256,8192]{2,1,0:T(8,128)(2,1)}), bf16[1,1024,8192]{2,1,0:T(8,128)(2,1)}) %all-gather.3.cloned.1.call-update) | async-done | bytes 16777232 | tf_op jit(solution)/shard_map/all_gather | solution.py:75
  118.2 2.6 fusion.20
  120.8 2.9 fusion.32
  123.7 3.2 %fusion.35 = f32[1024,256]{0,1:T(8,128)S(1)} fusion(f32[1024,256]{0,1:T(8,128)S(1)} %fusion.32, bf16[256,1024]{1,0:T(8,128)(2,1)} %collective-permute-done.1, bf16[1,1024,8192]{2,1,0:T(8,128)(2,1)} %all-gather.3.cloned.1.call-done, s32[]{:T(128)S(6)} %select_n.96), kind=kOutput, calls=%fused_computation.43 | convolution fusion | flops 537133056 | bytes 4718596 | tf_op jit(solution)/shard_map/sd,hd->sh/dot_general | solution.py:80
  126.9 2.4 fusion.38
  130.1 1.9 fusion.44
  132.0 1.8 fusion.47
  133.8 1.8 fusion.53
  136.0 3.8 %multiply_reduce_fusion.1 = (f32[2,512]{1,0:T(2,128)S(1)}, f32[2,512]{1,0:T(2,128)S(1)}, bf16[2,512,128]{2,1,0:T(8,128)(2,1)S(1)}) fusion(bf16[2,1024,128]{2,1,0:T(8,128)(2,1)S(1)} %bitcast.144, bf16[2,512,128]{2,1,0:T(8,128)(2,1)S(1)} %convolution_convert_fusion.1, bf16[1,1024,256]{2,1,0:T(8,128)(2,1)S(1)} %copy-done, s32[]{:T(128)S(6)} %select_n.89, ...), kind=kOutput, calls=%fused_computation.63 | convolution fusion | flops 273807360 | bytes 6041604 | tf_op jit(solution)/shard_map/hqk,kd->hqd/dot_general | solution.py:67
  140.0 12.7 %fusion = f32[256,8192]{1,0:T(8,128)} fusion(bf16[1024,256]{0,1:T(8,128)(2,1)S(1)} %bitcast.136, bf16[1,1024,8192]{2,1,0:T(8,128)(2,1)} %all-gather.3.cloned.1.call-done), kind=kOutput, calls=%fused_computation | convolution fusion | flops 4294967296 | bytes 25690112 | tf_op jit(solution)/shard_map/sh,sd->hd/dot_general | solution.py:87
  153.8 4.0 %multiply_convert_fusion = bf16[2,512,1024]{1,2,0:T(8,128)(2,1)S(1)} fusion(f32[1024,2,512]{2,0,1:T(8,128)} %copy-done.2, f32[2,512]{1,0:T(2,128)S(1)} %get-tuple-element.93, f32[2,512]{1,0:T(2,128)S(1)} %log_add_fusion, pred[512,1024]{0,1:T(8,128)(4,1)S(1)} %get-tuple-element.94, bf16[2,1024,128]{2,1,0:T(8,128)(2,1)S(1)} %bitcast.145, ...), kind=kOutput, calls=%fused_computation.4 | convolution fusion | flops 275775488 | bytes 7348228 | tf_op jit(solution)/shard_map/hqd,kd->hqk/dot_general | solution.py:102
  158.5 1.7 multiply_convert_fusion.1
  169.5 131.3 %reduce-scatter.2.cloned.1.call-done = f32[256,1024]{1,0:T(8,128)} async-done(((f32[256,8192]{1,0:T(8,128)}), f32[256,1024]{1,0:T(8,128)}) %reduce-scatter.2.cloned.1.call-update) | async-done | bytes 1048592 | tf_op jit(solution)/shard_map/reduce_scatter | solution.py:88
  (72 shorter events, 15.1 us)
Async XLA Ops:
  7.2 77.7 %copy-start = (bf16[1,1024,256]{2,1,0:T(8,128)(2,1)S(1)}, bf16[1,1024,256]{2,1,0:T(8,128)(2,1)}, u32[]{:S(2)}) copy-start(bf16[1,1024,256]{2,1,0:T(8,128)(2,1)} %param.24) | copy-start | bytes 1572868
  7.2 1.1 copy-start.12
  7.2 19.0 %copy-start.13 = (s32[1,4]{1,0:T(1,128)S(1)}, s32[1,4]{1,0:T(1,128)}, u32[]{:S(2)}) copy-start(s32[1,4]{1,0:T(1,128)} %param.27) | copy-start | bytes 52
  7.2 19.2 %copy-start.8 = (bf16[1,1024,256]{2,1,0:T(8,128)(2,1)S(1)}, bf16[1,1024,256]{2,1,0:T(8,128)(2,1)}, u32[]{:S(2)}) copy-start(bf16[1,1024,256]{2,1,0:T(8,128)(2,1)} %param.22) | copy-start | bytes 1572868
  7.2 111.0 %all-gather.3.cloned.1.call-start = ((), (), s32[]{:S(2)}) async-start(), calls=%async_computation.2 | async-start | bytes 20971520 | tf_op jit(solution)/shard_map/all_gather | solution.py:75
  7.9 292.9 %reduce-scatter.2.cloned.1.call-start = ((), (), s32[]{:S(2)}) async-start(), calls=%async_computation.1 | async-start | bytes 9437184 | tf_op jit(solution)/shard_map/reduce_scatter | solution.py:88
  8.3 18.0 %collective-permute-start = (bf16[256,1024]{1,0:T(8,128)(2,1)S(1)}, bf16[256,1024]{1,0:T(8,128)(2,1)S(1)}, u32[]{:S(2)}, u32[]{:S(2)}) collective-permute-start(bf16[256,1024]{1,0:T(8,128)(2,1)S(1)} %copy-done.12), channel_id=1, source_target_pairs={{0,4},{4,8},{8,12},{12,16},{16,20},{20,24},{24,28},{28,0},{1,5},{5... | collective-permute-start | bytes 1572872 | tf_op jit(solution)/shard_map/ppermute | solution.py:14
  26.2 15.9 %collective-permute-start.1 = (bf16[256,1024]{1,0:T(8,128)(2,1)S(1)}, bf16[256,1024]{1,0:T(8,128)(2,1)}, u32[]{:S(2)}, u32[]{:S(2)}) collective-permute-start(bf16[256,1024]{1,0:T(8,128)(2,1)S(1)} %collective-permute-done), channel_id=1, source_target_pairs={{0,4},{4,8},{8,12},{12,16},{16,20},{20,24},{24,28},{28,0},{1,5},{5... | collective-permute-start | bytes 1572872 | tf_op jit(solution)/shard_map/ppermute | solution.py:14
  42.1 15.1 %collective-permute-start.2 = (bf16[256,1024]{1,0:T(8,128)(2,1)}, bf16[256,1024]{1,0:T(8,128)(2,1)S(1)}, u32[]{:S(2)}, u32[]{:S(2)}) collective-permute-start(bf16[256,1024]{1,0:T(8,128)(2,1)} %collective-permute-done.1), channel_id=1, source_target_pairs={{0,4},{4,8},{8,12},{12,16},{16,20},{20,24},{24,28},{28,0},{1,5},{5... | collective-permute-start | bytes 1572872 | tf_op jit(solution)/shard_map/ppermute | solution.py:14
  57.3 14.1 %collective-permute-start.3 = (bf16[256,1024]{1,0:T(8,128)(2,1)S(1)}, bf16[256,1024]{1,0:T(8,128)(2,1)S(1)}, u32[]{:S(2)}, u32[]{:S(2)}) collective-permute-start(bf16[256,1024]{1,0:T(8,128)(2,1)S(1)} %collective-permute-done.2), channel_id=1, source_target_pairs={{0,4},{4,8},{8,12},{12,16},{16,20},{20,24},{24,28},{28,0},{1,5},{5... | collective-permute-start | bytes 1572872 | tf_op jit(solution)/shard_map/ppermute | solution.py:14
  59.1 14.2 %copy-start.2 = (f32[1024,2,512]{2,0,1:T(8,128)}, f32[1024,2,512]{2,0,1:T(8,128)S(1)}, u32[]{:S(2)}) copy-start(f32[1024,2,512]{2,0,1:T(8,128)S(1)} %get-tuple-element.101) | copy-start | bytes 12582916
  61.2 12.1 %copy-start.4 = (f32[1024,2,512]{2,0,1:T(8,128)}, f32[1024,2,512]{2,0,1:T(8,128)S(1)}, u32[]{:S(2)}) copy-start(f32[1024,2,512]{2,0,1:T(8,128)S(1)} %get-tuple-element.99) | copy-start | bytes 12582916
  71.3 2.0 copy-start.6
  71.3 13.3 %collective-permute-start.4 = (bf16[256,1024]{1,0:T(8,128)(2,1)S(1)}, bf16[256,1024]{1,0:T(8,128)(2,1)}, u32[]{:S(2)}, u32[]{:S(2)}) collective-permute-start(bf16[256,1024]{1,0:T(8,128)(2,1)S(1)} %collective-permute-done.3), channel_id=1, source_target_pairs={{0,4},{4,8},{8,12},{12,16},{16,20},{20,24},{24,28},{28,0},{1,5},{5... | collective-permute-start | bytes 1572872 | tf_op jit(solution)/shard_map/ppermute | solution.py:14
  84.7 12.7 %collective-permute-start.5 = (bf16[256,1024]{1,0:T(8,128)(2,1)}, bf16[256,1024]{1,0:T(8,128)(2,1)}, u32[]{:S(2)}, u32[]{:S(2)}) collective-permute-start(bf16[256,1024]{1,0:T(8,128)(2,1)} %collective-permute-done.4), channel_id=1, source_target_pairs={{0,4},{4,8},{8,12},{12,16},{16,20},{20,24},{24,28},{28,0},{1,5},{5... | collective-permute-start | bytes 1572872 | tf_op jit(solution)/shard_map/ppermute | solution.py:14
  97.3 36.5 %collective-permute-start.6 = (bf16[256,1024]{1,0:T(8,128)(2,1)}, bf16[256,1024]{1,0:T(8,128)(2,1)}, u32[]{:S(2)}, u32[]{:S(2)}) collective-permute-start(bf16[256,1024]{1,0:T(8,128)(2,1)} %collective-permute-done.5), channel_id=1, source_target_pairs={{0,4},{4,8},{8,12},{12,16},{16,20},{20,24},{24,28},{28,0},{1,5},{5... | collective-permute-start | bytes 1572872 | tf_op jit(solution)/shard_map/ppermute | solution.py:14
  118.2 11.0 %copy-start.1 = (bf16[1,1024,8192]{2,1,0:T(8,128)(2,1)S(1)}, bf16[1,1024,8192]{2,1,0:T(8,128)(2,1)}, u32[]{:S(2)}) copy-start(bf16[1,1024,8192]{2,1,0:T(8,128)(2,1)} %all-gather.3.cloned.1.call-done) | copy-start | bytes 50331652
  123.7 5.6 %copy-start.7 = (bf16[256,1024]{1,0:T(8,128)(2,1)S(1)}, bf16[256,1024]{1,0:T(8,128)(2,1)}, u32[]{:S(2)}) copy-start(bf16[256,1024]{1,0:T(8,128)(2,1)} %copy-done.6) | copy-start | bytes 1572868
  136.0 3.8 %copy-start.9 = (bf16[1024,2,128]{2,0,1:T(8,128)(2,1)}, bf16[1024,2,128]{2,0,1:T(8,128)(2,1)S(1)}, u32[]{:S(2)}) copy-start(bf16[1024,2,128]{2,0,1:T(8,128)(2,1)S(1)} %copy.31) | copy-start | bytes 1572868
  153.8 4.7 %copy-start.5 = (f32[1024,2,512]{2,0,1:T(8,128)S(1)}, f32[1024,2,512]{2,0,1:T(8,128)}, u32[]{:S(2)}) copy-start(f32[1024,2,512]{2,0,1:T(8,128)} %copy-done.4) | copy-start | bytes 12582916
  158.5 2.8 copy-start.11
  160.2 2.3 copy-start.3
  161.0 6.2 %collective-permute-start.7 = (f32[512,128]{1,0:T(8,128)S(1)}, f32[512,128]{1,0:T(8,128)S(1)}, u32[]{:S(2)}, u32[]{:S(2)}) collective-permute-start(f32[512,128]{1,0:T(8,128)S(1)} %constant_dynamic-slice_fusion.1), channel_id=1, source_target_pairs={{0,1},{1,0},{2,3},{3,2},{4,5},{5,4},{6,7},{7,6},{8,9},{9,8},{10,11... | collective-permute-start | bytes 786440 | tf_op jit(solution)/shard_map/ppermute | solution.py:24
  165.6 2.3 collective-permute-start.8
  (1 other events, 1.0 us)
Sparse Core Ops, SparseCore 0:
  9.6 108.6 all-gather.2
  152.9 147.8 reduce-scatter.1
